TPU v7x, 512 devices: a whole 4x8x8 slice. The times are simulated.
512 devices in a mesh: pipe: 32 (over z, y_hi), expert: 16 (over y_lo, x, core).
Axes of the slice: x: 4, y: 8 (y_hi: 4, y_lo: 2; y = y_hi * 2 + y_lo), z: 8, core: 2. Of those that a mesh axis runs over, the one named last changes fastest.
Arguments:
- tokens: bfloat16 [65536, 2048], P(('pipe', 'expert')), may hold values from -6 to 6
- cotangent: bfloat16 [65536, 2048], P(('pipe', 'expert')), may hold values from -6 to 6
- chosen: int32 [512, 64, 2], P(('pipe', 'expert')), may hold values from 0 to 127, as said below
- gate_value: bfloat16 [512, 64, 2], P(('pipe', 'expert')), may hold values from 0.049804688 to 1
- gate_weight: bfloat16 [2048, 65536], P(None, ('pipe', 'expert')), may hold values from -0.125 to 0.125
- up_weight: bfloat16 [2048, 65536], P(None, ('pipe', 'expert')), may hold values from -0.125 to 0.125
- down_weight: bfloat16 [65536, 2048], P(('pipe', 'expert')), may hold values from -0.1875 to 0.1875
Outputs:
- token_grad: bfloat16 [65536, 2048], P(('pipe', 'expert'))
- gate_grad: float32 [512, 64, 2], P(('pipe', 'expert'))
- gate_weight_grad: bfloat16 [2048, 65536], P(None, ('pipe', 'expert'))
- up_weight_grad: bfloat16 [2048, 65536], P(None, ('pipe', 'expert'))
- down_weight_grad: bfloat16 [65536, 2048], P(('pipe', 'expert'))
Inputs may be any that keep to these rules, and one draw needn't show every extreme that they name: `chosen`: for each routing group and expert, the 2 entries are different token indices within that group's 128 tokens.
All inputs are finite; a program needn't handle non-finite values.
Results may differ from a plain program's by a relative error of at most 0.0095.
Values may be sent and summed in bfloat16 or wider, within the bound.
No kernel may reach another device: no remote copies, remote signals or barrier semaphores. Data moves between devices by JAX's collectives and lax.ppermute only.
A program may use at most 128 MiB of HBM per device.

v0:
```python
import jax
import jax.numpy as jnp
from jax import lax
from jax.sharding import PartitionSpec as P


def select_rows(tokens, cotangent, list_flat):
    picked = jnp.take(tokens, list_flat, axis=0)
    dpicked = jnp.take(cotangent, list_flat, axis=0)
    return (picked, dpicked)


def expert_work(rows_x, rows_dy, rows_gate, gate_weight, up_weight, down_weight):
    feature_width = rows_x.shape[-1]
    picked = rows_x.reshape(-1, feature_width)
    dpicked = rows_dy.reshape(-1, feature_width)
    factor = rows_gate.reshape(-1).astype(jnp.float32)[:, None]
    contract_rows = (((0,), (0,)), ((), ()))
    contract_units = (((1,), (1,)), ((), ()))
    gate_pre = jnp.dot(picked, gate_weight, preferred_element_type=jnp.float32)
    up_pre = jnp.dot(picked, up_weight, preferred_element_type=jnp.float32)
    back = lax.dot_general(dpicked, down_weight, contract_units, preferred_element_type=jnp.float32)
    logistic = jax.nn.sigmoid(gate_pre)
    activated = gate_pre * logistic
    hidden = (activated * up_pre).astype(jnp.bfloat16)
    router = jnp.sum(hidden.astype(jnp.float32) * back, axis=1)
    hidden_grad = factor * back
    gate_pre_grad = (hidden_grad * up_pre * logistic * (1.0 + gate_pre * (1.0 - logistic))).astype(
        jnp.bfloat16
    )
    up_pre_grad = (hidden_grad * activated).astype(jnp.bfloat16)
    scaled = (factor * dpicked.astype(jnp.float32)).astype(jnp.bfloat16)
    down_grad = lax.dot_general(
        hidden, scaled, contract_rows, preferred_element_type=jnp.float32
    ).astype(jnp.bfloat16)
    gate_grad_w = lax.dot_general(
        picked, gate_pre_grad, contract_rows, preferred_element_type=jnp.float32
    ).astype(jnp.bfloat16)
    up_grad_w = lax.dot_general(
        picked, up_pre_grad, contract_rows, preferred_element_type=jnp.float32
    ).astype(jnp.bfloat16)
    block_grad = lax.dot_general(
        gate_pre_grad, gate_weight, contract_units, preferred_element_type=jnp.float32
    )
    block_grad = block_grad + lax.dot_general(
        up_pre_grad, up_weight, contract_units, preferred_element_type=jnp.float32
    )
    return (block_grad.astype(jnp.bfloat16), router, gate_grad_w, up_grad_w, down_grad)


def per_device(tokens, cotangent, chosen, gate_value, gate_weight, up_weight, down_weight):
    column_count = lax.axis_size("expert")
    pipe_count = lax.axis_size("pipe")
    block_count = min(8, column_count)
    per_pipe = column_count // block_count
    pick_count = chosen.shape[2]
    feature_width = tokens.shape[1]
    my_column = lax.axis_index("expert")
    list_flat = chosen[0].reshape(-1)
    picked, dpicked = select_rows(tokens, cotangent, list_flat)
    sent_x = picked.reshape(pipe_count, per_pipe, pick_count, feature_width)
    sent_dy = dpicked.reshape(pipe_count, per_pipe, pick_count, feature_width)
    sent_gate = gate_value[0].reshape(pipe_count, per_pipe, pick_count)
    got_x, got_dy, got_gate = (
        lax.all_to_all(sent_x, "pipe", split_axis=0, concat_axis=0, tiled=True),
        lax.all_to_all(sent_dy, "pipe", split_axis=0, concat_axis=0, tiled=True),
        lax.all_to_all(sent_gate, "pipe", split_axis=0, concat_axis=0, tiled=True),
    )
    wide_x = jnp.repeat(got_x, block_count, axis=1)
    wide_dy = jnp.repeat(got_dy, block_count, axis=1)
    wide_gate = jnp.repeat(got_gate, block_count, axis=1)
    rows_x, rows_dy, rows_gate = (
        lax.all_to_all(wide_x, "expert", split_axis=1, concat_axis=1, tiled=True),
        lax.all_to_all(wide_dy, "expert", split_axis=1, concat_axis=1, tiled=True),
        lax.all_to_all(wide_gate, "expert", split_axis=1, concat_axis=1, tiled=True),
    )
    block_grad, router, gate_weight_grad, up_weight_grad, down_weight_grad = expert_work(
        rows_x, rows_dy, rows_gate, gate_weight, up_weight, down_weight
    )
    my_expert = my_column // block_count
    router_grid = router.reshape(1, pipe_count, column_count, pick_count)
    expert_slots = jnp.arange(per_pipe, dtype=jnp.int32)[:, None, None, None]
    placed_router = jnp.where(expert_slots == my_expert, router_grid, jnp.float32(0.0))
    router_totals = lax.psum(placed_router, "expert")
    router_mine = lax.dynamic_index_in_dim(router_totals, my_column, axis=2, keepdims=False)
    router_home = jnp.transpose(router_mine, (1, 0, 2))
    returned = lax.all_to_all(
        block_grad.reshape(pipe_count, column_count, pick_count, feature_width),
        "expert",
        split_axis=1,
        concat_axis=1,
        tiled=True,
    )
    summed = jnp.sum(
        returned.astype(jnp.float32).reshape(
            pipe_count, per_pipe, block_count, pick_count, feature_width
        ),
        axis=2,
    )
    home_rows, home_router = (
        lax.all_to_all(summed, "pipe", split_axis=0, concat_axis=0, tiled=True),
        lax.all_to_all(router_home, "pipe", split_axis=0, concat_axis=0, tiled=True),
    )
    flat_rows = home_rows.reshape(-1, feature_width)
    columns = jnp.arange(tokens.shape[0], dtype=jnp.int32)
    onehot = (list_flat[:, None] == columns[None, :]).astype(jnp.float32)
    token_grad = lax.dot_general(
        onehot,
        flat_rows,
        (((0,), (0,)), ((), ())),
        precision=lax.Precision.HIGHEST,
        preferred_element_type=jnp.float32,
    ).astype(jnp.bfloat16)
    gate_grad = home_router.reshape(1, -1, pick_count)
    return (token_grad, gate_grad, gate_weight_grad, up_weight_grad, down_weight_grad)


def solution(mesh):
    return jax.shard_map(
        per_device,
        mesh=mesh,
        in_specs=(
            P(("pipe", "expert"), None),
            P(("pipe", "expert"), None),
            P(("pipe", "expert"), None, None),
            P(("pipe", "expert"), None, None),
            P(None, ("pipe", "expert")),
            P(None, ("pipe", "expert")),
            P(("pipe", "expert"), None),
        ),
        out_specs=(
            P(("pipe", "expert"), None),
            P(("pipe", "expert"), None, None),
            P(None, ("pipe", "expert")),
            P(None, ("pipe", "expert")),
            P(("pipe", "expert"), None),
        ),
        check_vma=False,
    )
```

profile of v0, /device:TPU:87, one launch (start us, length us, event | category | flops | bytes accessed | tf_op | source)
XLA Modules:
  0.0 450.7 jit_solution(946452296318267621)
XLA Ops:
  0.6 0.0 copy-start
  0.6 0.0 copy-start.4
  0.7 0.9 reshape_squeeze.4
  1.5 0.6 copy.80
  2.1 14.6 %all-to-all-start = ((bf16[32,2,2]{1,2,0:T(2,128)(2,1)}), bf16[32,2,2]{1,2,0:T(2,128)(2,1)S(1)}, u32[]{:S(2)}, u32[]{:S(2)}) async-start(bf16[32,2,2]{1,2,0:T(2,128)(2,1)} %copy.80), calls=%async_computation | async-start | bytes 32768 | tf_op jit(solution)/shard_map/all_to_all | solution.py:67
  16.7 0.8 copy.79
  17.5 0.1 eq.26
  17.7 2.6 gather_fusion.1
  20.3 0.9 gather_fusion
  21.2 3.8 all-to-all-done
  25.0 0.1 copy.81
  25.1 0.6 broadcast_in_dim.43
  25.7 6.7 %all-to-all-start.1 = ((bf16[32,16,2]{0,2,1:T(2,128)(2,1)}), bf16[32,16,2]{0,2,1:T(2,128)(2,1)S(1)}, u32[]{:S(2)}, u32[]{:S(2)}) async-start(bf16[32,16,2]{0,2,1:T(2,128)(2,1)} %bitcast), calls=%async_computation.1 | async-start | bytes 16384 | tf_op jit(solution)/shard_map/all_to_all | solution.py:75
  32.4 0.2 broadcast_select_fusion.1
  32.5 1.1 reshape.71
  33.7 2.5 all-to-all-done.1
  36.2 6.9 %all-to-all-start.4 = ((bf16[32,2,2,2048]{3,2,1,0:T(2,128)(2,1)}), bf16[32,2,2,2048]{3,2,1,0:T(2,128)(2,1)S(1)}, u32[]{:S(2)}, u32[]{:S(2)}) async-start(bf16[32,2,2,2048]{3,2,1,0:T(2,128)(2,1)} %reshape.71), calls=%async_computation.4 | async-start | bytes 1048576 | tf_op jit(solution)/shard_map/all_to_all | solution.py:65
  43.1 1.1 reshape.68
  44.2 18.4 %all-to-all-done.4 = bf16[32,2,2,2048]{3,2,1,0:T(2,128)(2,1)S(1)} async-done(((bf16[32,2,2,2048]{3,2,1,0:T(2,128)(2,1)}), bf16[32,2,2,2048]{3,2,1,0:T(2,128)(2,1)S(1)}, u32[]{:S(2)}, u32[]{:S(2)}) %all-to-all-start.4) | async-done | bytes 524320 | tf_op jit(solution)/shard_map/all_to_all | solution.py:65
  62.6 6.6 %all-to-all-start.2 = ((bf16[32,2,2,2048]{3,2,1,0:T(2,128)(2,1)}), bf16[32,2,2,2048]{3,2,1,0:T(2,128)(2,1)S(1)}, u32[]{:S(2)}, u32[]{:S(2)}) async-start(bf16[32,2,2,2048]{3,2,1,0:T(2,128)(2,1)} %reshape.68), calls=%async_computation.2 | async-start | bytes 1048576 | tf_op jit(solution)/shard_map/all_to_all | solution.py:66
  69.2 0.4 copy.86
  69.5 17.4 %all-to-all-done.2 = bf16[32,2,2,2048]{3,2,1,0:T(2,128)(2,1)S(1)} async-done(((bf16[32,2,2,2048]{3,2,1,0:T(2,128)(2,1)}), bf16[32,2,2,2048]{3,2,1,0:T(2,128)(2,1)S(1)}, u32[]{:S(2)}, u32[]{:S(2)}) %all-to-all-start.2) | async-done | bytes 524320 | tf_op jit(solution)/shard_map/all_to_all | solution.py:66
  87.0 5.5 %broadcast_in_dim.45 = bf16[32,2,8,2,2048]{4,3,0,2,1:T(2,128)(2,1)} broadcast(bf16[32,2,2,2048]{3,2,0,1:T(2,128)(2,1)S(1)} %copy.86), dimensions={0,1,3,4} | broadcast | bytes 4718592 | tf_op jit(solution)/shard_map/broadcast_in_dim | solution.py:69
  92.5 7.1 %all-to-all-start.5 = ((bf16[32,16,2,2048]{3,2,0,1:T(2,128)(2,1)}), bf16[32,16,2,2048]{3,2,0,1:T(2,128)(2,1)}, u32[]{:S(2)}, u32[]{:S(2)}) async-start(bf16[32,16,2,2048]{3,2,0,1:T(2,128)(2,1)} %bitcast.30), calls=%async_computation.5 | async-start | bytes 8388608 | tf_op jit(solution)/shard_map/all_to_all | solution.py:73
  99.6 0.4 copy.84
  100.0 61.0 %all-to-all-done.5 = bf16[32,16,2,2048]{3,2,0,1:T(2,128)(2,1)} async-done(((bf16[32,16,2,2048]{3,2,0,1:T(2,128)(2,1)}), bf16[32,16,2,2048]{3,2,0,1:T(2,128)(2,1)}, u32[]{:S(2)}, u32[]{:S(2)}) %all-to-all-start.5) | async-done | bytes 4194336 | tf_op jit(solution)/shard_map/all_to_all | solution.py:73
  160.9 5.5 %broadcast_in_dim.44 = bf16[32,2,8,2,2048]{4,3,0,2,1:T(2,128)(2,1)} broadcast(bf16[32,2,2,2048]{3,2,0,1:T(2,128)(2,1)S(1)} %copy.84), dimensions={0,1,3,4} | broadcast | bytes 4718592 | tf_op jit(solution)/shard_map/broadcast_in_dim | solution.py:70
  166.4 5.9 %all-to-all-start.3 = ((bf16[32,16,2,2048]{3,2,0,1:T(2,128)(2,1)}), bf16[32,16,2,2048]{3,2,0,1:T(2,128)(2,1)}, u32[]{:S(2)}, u32[]{:S(2)}) async-start(bf16[32,16,2,2048]{3,2,0,1:T(2,128)(2,1)} %bitcast.29), calls=%async_computation.3 | async-start | bytes 8388608 | tf_op jit(solution)/shard_map/all_to_all | solution.py:74
  172.3 0.2 copy.83
  172.5 0.2 reshape.79
  172.7 8.6 %copy.87 = bf16[32,16,2,2048]{3,2,1,0:T(2,128)(2,1)} copy(bf16[32,16,2,2048]{3,2,0,1:T(2,128)(2,1)} %all-to-all-done.5) | data formatting | bytes 8388608 | tf_op jit(solution)/shard_map/all_to_all | solution.py:73
  181.4 7.2 %reshape.73 = bf16[1024,2048]{1,0:T(8,128)(2,1)} reshape(bf16[32,16,2,2048]{3,2,1,0:T(2,128)(2,1)} %copy.87) | data formatting | bytes 8388608 | tf_op jit(solution)/shard_map/reshape | solution.py:15
  188.6 3.9 fusion.6
  192.4 1.5 fusion.5
  194.0 39.6 %all-to-all-done.3 = bf16[32,16,2,2048]{3,2,0,1:T(2,128)(2,1)} async-done(((bf16[32,16,2,2048]{3,2,0,1:T(2,128)(2,1)}), bf16[32,16,2,2048]{3,2,0,1:T(2,128)(2,1)}, u32[]{:S(2)}, u32[]{:S(2)}) %all-to-all-start.3) | async-done | bytes 4194336 | tf_op jit(solution)/shard_map/all_to_all | solution.py:74
  233.6 8.7 %copy.85 = bf16[32,16,2,2048]{3,2,1,0:T(2,128)(2,1)} copy(bf16[32,16,2,2048]{3,2,0,1:T(2,128)(2,1)} %all-to-all-done.3) | data formatting | bytes 8388608 | tf_op jit(solution)/shard_map/all_to_all | solution.py:74
  242.3 7.5 %reshape.70 = bf16[1024,2048]{1,0:T(8,128)(2,1)} reshape(bf16[32,16,2,2048]{3,2,1,0:T(2,128)(2,1)} %copy.85) | data formatting | bytes 8388608 | tf_op jit(solution)/shard_map/reshape | solution.py:16
  249.7 3.9 multiply_reduce_fusion
  253.6 1.3 fusion.7
  254.9 3.2 add_convert_fusion
  258.1 7.7 %reshape.74 = bf16[32,16,2,2048]{3,2,1,0:T(2,128)(2,1)} reshape(bf16[1024,2048]{1,0:T(8,128)(2,1)} %add_convert_fusion) | data formatting | bytes 8388608 | tf_op jit(solution)/shard_map/reshape | solution.py:88
  265.8 8.0 %copy.88 = bf16[32,16,2,2048]{3,2,0,1:T(2,128)(2,1)} copy(bf16[32,16,2,2048]{3,2,1,0:T(2,128)(2,1)} %reshape.74) | data formatting | bytes 8388608 | tf_op jit(solution)/shard_map/reshape | solution.py:88
  273.8 5.9 %all-to-all-start.6 = ((bf16[32,16,2,2048]{3,2,0,1:T(2,128)(2,1)}), bf16[32,16,2,2048]{3,2,0,1:T(2,128)(2,1)}, u32[]{:S(2)}, u32[]{:S(2)}) async-start(bf16[32,16,2,2048]{3,2,0,1:T(2,128)(2,1)} %copy.88), calls=%async_computation.6 | async-start | bytes 8388608 | tf_op jit(solution)/shard_map/all_to_all | solution.py:87
  279.7 0.2 broadcast_in_dim.47
  279.9 0.2 copy.90
  280.1 0.1 broadcast_select_fusion.2
  280.2 101.7 %psum.7 = f32[2,32,16,2]{1,3,2,0:T(2,128)S(1)} all-reduce(f32[2,32,16,2]{1,3,2,0:T(2,128)S(1)} %broadcast_select_fusion.2), channel_id=1, replica_groups=mesh['pipe'=32,'expert'=16] {'expert'}, use_global_device_ids=true, to_apply=%region_2.4 | all-reduce | flops 2048 | bytes 16384 | tf_op jit(solution)/shard_map/psum | solution.py:84
  381.9 0.7 copy.91
  382.7 0.0 all-to-all-done.6
  382.7 6.6 %all-to-all-start.8 = ((f32[32,2,2]{2,1,0:T(2,128)}), f32[32,2,2]{2,1,0:T(2,128)S(1)}, u32[]{:S(2)}, u32[]{:S(2)}) async-start(f32[32,2,2]{2,1,0:T(2,128)} %copy.91), calls=%async_computation.8 | async-start | bytes 65536 | tf_op jit(solution)/shard_map/all_to_all | solution.py:102
  389.2 6.3 %convert_reduce_fusion = f32[32,2,2,2048]{3,2,0,1:T(2,128)S(1)} fusion(bf16[32,16,2,2048]{3,2,0,1:T(2,128)(2,1)} %all-to-all-done.6), kind=kLoop, calls=%fused_computation.2 | loop fusion | flops 3932160 | bytes 5242880 | tf_op jit(solution)/shard_map/reduce_sum | solution.py:94
  395.6 1.1 copy.89
  396.7 0.9 all-to-all-done.8
  397.6 10.8 %all-to-all-start.7 = ((f32[32,2,2,2048]{3,2,1,0:T(2,128)}), f32[32,2,2,2048]{3,2,1,0:T(2,128)S(1)}, u32[]{:S(2)}, u32[]{:S(2)}) async-start(f32[32,2,2,2048]{3,2,1,0:T(2,128)} %copy.89), calls=%async_computation.7 | async-start | bytes 2097152 | tf_op jit(solution)/shard_map/all_to_all | solution.py:101
  408.3 0.0 copy-start.3
  408.3 0.0 copy-start.5
  408.4 4.4 convolution_convert_fusion.1
  412.8 0.0 copy-done.3
  412.8 2.1 convolution_convert_fusion
  414.9 1.9 fusion.2
  416.8 0.6 copy.93
  417.4 30.8 %all-to-all-done.7 = f32[32,2,2,2048]{3,2,1,0:T(2,128)S(1)} async-done(((f32[32,2,2,2048]{3,2,1,0:T(2,128)}), f32[32,2,2,2048]{3,2,1,0:T(2,128)S(1)}, u32[]{:S(2)}, u32[]{:S(2)}) %all-to-all-start.7) | async-done | bytes 1048608 | tf_op jit(solution)/shard_map/all_to_all | solution.py:101
  448.2 0.7 reshape.77
  449.0 1.5 convolution_convert_fusion.2
  (17 shorter events, 0.1 us)
Async XLA Ops:
  0.6 187.9 %copy-start = (bf16[2048,128]{1,0:T(8,128)(2,1)S(1)}, bf16[2048,128]{1,0:T(8,128)(2,1)}, u32[]{:S(2)}) copy-start(bf16[2048,128]{1,0:T(8,128)(2,1)} %param.13) | copy-start | bytes 1572868
  0.6 19.6 %copy-start.4 = (bf16[128,2048]{1,0:T(8,128)(2,1)S(1)}, bf16[128,2048]{1,0:T(8,128)(2,1)}, u32[]{:S(2)}) copy-start(bf16[128,2048]{1,0:T(8,128)(2,1)} %param.10) | copy-start | bytes 1572868
  2.1 22.9 %all-to-all-start = ((bf16[32,2,2]{1,2,0:T(2,128)(2,1)}), bf16[32,2,2]{1,2,0:T(2,128)(2,1)S(1)}, u32[]{:S(2)}, u32[]{:S(2)}) async-start(bf16[32,2,2]{1,2,0:T(2,128)(2,1)} %copy.80), calls=%async_computation | async-start | bytes 32768 | tf_op jit(solution)/shard_map/all_to_all | solution.py:67
  25.7 10.4 %all-to-all-start.1 = ((bf16[32,16,2]{0,2,1:T(2,128)(2,1)}), bf16[32,16,2]{0,2,1:T(2,128)(2,1)S(1)}, u32[]{:S(2)}, u32[]{:S(2)}) async-start(bf16[32,16,2]{0,2,1:T(2,128)(2,1)} %bitcast), calls=%async_computation.1 | async-start | bytes 16384 | tf_op jit(solution)/shard_map/all_to_all | solution.py:75
  36.2 26.4 %all-to-all-start.4 = ((bf16[32,2,2,2048]{3,2,1,0:T(2,128)(2,1)}), bf16[32,2,2,2048]{3,2,1,0:T(2,128)(2,1)S(1)}, u32[]{:S(2)}, u32[]{:S(2)}) async-start(bf16[32,2,2,2048]{3,2,1,0:T(2,128)(2,1)} %reshape.71), calls=%async_computation.4 | async-start | bytes 1048576 | tf_op jit(solution)/shard_map/all_to_all | solution.py:65
  62.6 24.4 %all-to-all-start.2 = ((bf16[32,2,2,2048]{3,2,1,0:T(2,128)(2,1)}), bf16[32,2,2,2048]{3,2,1,0:T(2,128)(2,1)S(1)}, u32[]{:S(2)}, u32[]{:S(2)}) async-start(bf16[32,2,2,2048]{3,2,1,0:T(2,128)(2,1)} %reshape.68), calls=%async_computation.2 | async-start | bytes 1048576 | tf_op jit(solution)/shard_map/all_to_all | solution.py:66
  92.5 68.5 %all-to-all-start.5 = ((bf16[32,16,2,2048]{3,2,0,1:T(2,128)(2,1)}), bf16[32,16,2,2048]{3,2,0,1:T(2,128)(2,1)}, u32[]{:S(2)}, u32[]{:S(2)}) async-start(bf16[32,16,2,2048]{3,2,0,1:T(2,128)(2,1)} %bitcast.30), calls=%async_computation.5 | async-start | bytes 8388608 | tf_op jit(solution)/shard_map/all_to_all | solution.py:73
  166.4 67.1 %all-to-all-start.3 = ((bf16[32,16,2,2048]{3,2,0,1:T(2,128)(2,1)}), bf16[32,16,2,2048]{3,2,0,1:T(2,128)(2,1)}, u32[]{:S(2)}, u32[]{:S(2)}) async-start(bf16[32,16,2,2048]{3,2,0,1:T(2,128)(2,1)} %bitcast.29), calls=%async_computation.3 | async-start | bytes 8388608 | tf_op jit(solution)/shard_map/all_to_all | solution.py:74
  188.6 3.9 copy-start.2
  188.6 3.9 copy-start.6
  242.3 7.5 %copy-start.7 = (bf16[128,2048]{1,0:T(8,128)(2,1)S(1)}, bf16[128,2048]{1,0:T(8,128)(2,1)}, u32[]{:S(2)}) copy-start(bf16[128,2048]{1,0:T(8,128)(2,1)} %param.15) | copy-start | bytes 1572868
  273.8 108.9 %all-to-all-start.6 = ((bf16[32,16,2,2048]{3,2,0,1:T(2,128)(2,1)}), bf16[32,16,2,2048]{3,2,0,1:T(2,128)(2,1)}, u32[]{:S(2)}, u32[]{:S(2)}) async-start(bf16[32,16,2,2048]{3,2,0,1:T(2,128)(2,1)} %copy.88), calls=%async_computation.6 | async-start | bytes 8388608 | tf_op jit(solution)/shard_map/all_to_all | solution.py:87
  382.7 14.9 %all-to-all-start.8 = ((f32[32,2,2]{2,1,0:T(2,128)}), f32[32,2,2]{2,1,0:T(2,128)S(1)}, u32[]{:S(2)}, u32[]{:S(2)}) async-start(f32[32,2,2]{2,1,0:T(2,128)} %copy.91), calls=%async_computation.8 | async-start | bytes 65536 | tf_op jit(solution)/shard_map/all_to_all | solution.py:102
  397.6 50.7 %all-to-all-start.7 = ((f32[32,2,2,2048]{3,2,1,0:T(2,128)}), f32[32,2,2,2048]{3,2,1,0:T(2,128)S(1)}, u32[]{:S(2)}, u32[]{:S(2)}) async-start(f32[32,2,2,2048]{3,2,1,0:T(2,128)} %copy.89), calls=%async_computation.7 | async-start | bytes 2097152 | tf_op jit(solution)/shard_map/all_to_all | solution.py:101
  408.3 4.5 copy-start.3
  408.3 6.6 %copy-start.5 = (bf16[1024,2048]{1,0:T(8,128)(2,1)S(1)}, bf16[1024,2048]{1,0:T(8,128)(2,1)}, u32[]{:S(2)}) copy-start(bf16[1024,2048]{1,0:T(8,128)(2,1)} %reshape.70) | copy-start | bytes 12582916
  414.9 35.6 %copy-start.1 = (bf16[2048,128]{1,0:T(8,128)(2,1)S(1)}, bf16[2048,128]{1,0:T(8,128)(2,1)}, u32[]{:S(2)}) copy-start(bf16[2048,128]{1,0:T(8,128)(2,1)} %param.13) | copy-start | bytes 1572868
where the time goes:
time: 459 us; the launch traced here: 451 us
  waiting for transfers between devices  174 us (38%)
  blocking collectives  102 us (22%)
  local copies, waits for them, and re-layouts  72.2 us (16%)
  starting transfers between devices  71.1 us (15%)
  matrix products  23.7 us (5%)
  other arithmetic  6.59 us (1%)
    psum x1, blocking collectives, per_device(): router_totals = lax.psum(placed_router, 'expert')  102 us
    all_to_all x1, waiting for transfers between devices, per_device(): lax.all_to_all(wide_x, 'expert', split_axis=1, concat_axis=1, tiled=True)  61 us
    all_to_all x1, waiting for transfers between devices, per_device(): lax.all_to_all(wide_dy, 'expert', split_axis=1, concat_axis=1, tiled=True)  39.6 us
    all_to_all x1, waiting for transfers between devices, per_device(): lax.all_to_all(summed, 'pipe', split_axis=0, concat_axis=0, tiled=True)  30.8 us
    all_to_all x1, waiting for transfers between devices, per_device(): lax.all_to_all(sent_x, 'pipe', split_axis=0, concat_axis=0, tiled=True)  18.4 us
    all_to_all x1, waiting for transfers between devices, per_device(): lax.all_to_all(sent_dy, 'pipe', split_axis=0, concat_axis=0, tiled=True)  17.4 us
    reshape x2, local copies, waits for them, and re-layouts, per_device(): block_grad.reshape(pipe_count, column_count, pick_count, feature_width)  15.7 us
    all_to_all x1, starting transfers between devices, per_device(): lax.all_to_all(sent_gate, 'pipe', split_axis=0, concat_axis=0, tiled=True)  14.6 us
  transfers between devices with their start and end apart: 9, of which 8 were waited for; matrix products, arithmetic and copies ran while one was open for 10% of the time, Pallas kernels for 0%

commit v1 on v0

--- a/solution.py
+++ b/solution.py
@@ -2,6 +2,18 @@
 import jax.numpy as jnp
 from jax import lax
 from jax.sharding import PartitionSpec as P
+
+
+def waves_report(xx):
+    return jnp.concatenate(
+        lax.all_to_all(
+            jnp.stack(jnp.split(xx, lax.psum(1, axis_name="expert"), axis=1), axis=0),
+            "expert",
+            0,
+            0,
+        ),
+        axis=1,
+    )
 
 
 def select_rows(tokens, cotangent, list_flat):
@@ -70,7 +82,7 @@
     wide_dy = jnp.repeat(got_dy, block_count, axis=1)
     wide_gate = jnp.repeat(got_gate, block_count, axis=1)
     rows_x, rows_dy, rows_gate = (
-        lax.all_to_all(wide_x, "expert", split_axis=1, concat_axis=1, tiled=True),
+        waves_report(wide_x),
         lax.all_to_all(wide_dy, "expert", split_axis=1, concat_axis=1, tiled=True),
         lax.all_to_all(wide_gate, "expert", split_axis=1, concat_axis=1, tiled=True),
     )

time: 459 us -> 456 us (level)
  local copies, waits for them, and re-layouts: 72.2 us -> 84.2 us
  waiting for transfers between devices: 174 us -> 162 us
    all_to_all x1, waiting for transfers between devices: 61 us -> 45 us  [waves_report(): lax.all_to_all(jnp.stack(jnp.split(xx, lax.psum(1, axis_name='expert'), a...]
    unnamed x17 -> x32, local copies, waits for them, and re-layouts: 0.81 us -> 14.1 us
    all_to_all x1 -> x0, local copies, waits for them, and re-layouts: 8.64 us -> none  [per_device(): lax.all_to_all(wide_x, 'expert', split_axis=1, concat_axis=1, tiled=True)]
    another operation x0 -> x2, local copies, waits for them, and re-layouts: none -> 8.34 us  [the longest x1 7.46 us: expert_work(): picked = rows_x.reshape(-1, feature_width)]
  transfers between devices with their start and end apart: 9 -> 9, of which waited for: 8 -> 8; matrix products, arithmetic and copies ran while one was open for 10% -> 13% of each run, Pallas kernels for 0% -> 0%
where the time goes in v1:
time: 456 us; the launch traced here: 449 us
  waiting for transfers between devices  162 us (36%)
  blocking collectives  102 us (22%)
  local copies, waits for them, and re-layouts  84.2 us (18%)
  starting transfers between devices  71.6 us (16%)
  matrix products  21.6 us (5%)
  other arithmetic  6.59 us (1%)
    psum x1, blocking collectives, per_device(): router_totals = lax.psum(placed_router, 'expert')  102 us
    all_to_all x1, waiting for transfers between devices, waves_report(): lax.all_to_all(jnp.stack(jnp.split(xx, lax.psum(1, axis_name='expert'), a...  45 us
    all_to_all x1, waiting for transfers between devices, per_device(): lax.all_to_all(wide_dy, 'expert', split_axis=1, concat_axis=1, tiled=True)  43.4 us
    all_to_all x1, waiting for transfers between devices, per_device(): lax.all_to_all(summed, 'pipe', split_axis=0, concat_axis=0, tiled=True)  30.8 us
    all_to_all x1, waiting for transfers between devices, per_device(): lax.all_to_all(sent_dy, 'pipe', split_axis=0, concat_axis=0, tiled=True)  18.4 us
    all_to_all x1, waiting for transfers between devices, per_device(): lax.all_to_all(sent_x, 'pipe', split_axis=0, concat_axis=0, tiled=True)  17.4 us
    reshape x2, local copies, waits for them, and re-layouts, per_device(): block_grad.reshape(pipe_count, column_count, pick_count, feature_width)  15.7 us
    all_to_all x1, starting transfers between devices, per_device(): lax.all_to_all(sent_gate, 'pipe', split_axis=0, concat_axis=0, tiled=True)  14.6 us
  transfers between devices with their start and end apart: 9, of which 8 were waited for; matrix products, arithmetic and copies ran while one was open for 13% of the time, Pallas kernels for 0%

profile of v1, /device:TPU:87, one launch (start us, length us, event | category | flops | bytes accessed | tf_op | source)
XLA Modules:
  0.0 449.0 jit_solution(3630337077148495641)
XLA Ops:
  0.7 0.9 reshape_squeeze.4
  1.5 0.6 copy.112
  2.1 14.6 %all-to-all-start = ((bf16[32,2,2]{1,2,0:T(2,128)(2,1)}), bf16[32,2,2]{1,2,0:T(2,128)(2,1)S(1)}, u32[]{:S(2)}, u32[]{:S(2)}) async-start(bf16[32,2,2]{1,2,0:T(2,128)(2,1)} %copy.112), calls=%async_computation | async-start | bytes 32768 | tf_op jit(solution)/shard_map/all_to_all | solution.py:79
  16.7 0.8 copy.111
  17.7 2.6 gather_fusion.1
  20.3 0.9 gather_fusion
  21.2 3.8 all-to-all-done
  25.1 0.6 broadcast_in_dim.43
  25.7 6.7 %all-to-all-start.1 = ((bf16[32,16,2]{0,2,1:T(2,128)(2,1)}), bf16[32,16,2]{0,2,1:T(2,128)(2,1)S(1)}, u32[]{:S(2)}, u32[]{:S(2)}) async-start(bf16[32,16,2]{0,2,1:T(2,128)(2,1)} %bitcast), calls=%async_computation.1 | async-start | bytes 16384 | tf_op jit(solution)/shard_map/all_to_all | solution.py:87
  32.5 1.1 reshape.68
  33.7 2.5 all-to-all-done.1
  36.1 6.9 %all-to-all-start.2 = ((bf16[32,2,2,2048]{3,2,1,0:T(2,128)(2,1)}), bf16[32,2,2,2048]{3,2,1,0:T(2,128)(2,1)S(1)}, u32[]{:S(2)}, u32[]{:S(2)}) async-start(bf16[32,2,2,2048]{3,2,1,0:T(2,128)(2,1)} %reshape.68), calls=%async_computation.2 | async-start | bytes 1048576 | tf_op jit(solution)/shard_map/all_to_all | solution.py:78
  43.1 1.1 reshape.71
  44.2 18.4 %all-to-all-done.2 = bf16[32,2,2,2048]{3,2,1,0:T(2,128)(2,1)S(1)} async-done(((bf16[32,2,2,2048]{3,2,1,0:T(2,128)(2,1)}), bf16[32,2,2,2048]{3,2,1,0:T(2,128)(2,1)S(1)}, u32[]{:S(2)}, u32[]{:S(2)}) %all-to-all-start.2) | async-done | bytes 524320 | tf_op jit(solution)/shard_map/all_to_all | solution.py:78
  62.6 6.6 %all-to-all-start.4 = ((bf16[32,2,2,2048]{3,2,1,0:T(2,128)(2,1)}), bf16[32,2,2,2048]{3,2,1,0:T(2,128)(2,1)S(1)}, u32[]{:S(2)}, u32[]{:S(2)}) async-start(bf16[32,2,2,2048]{3,2,1,0:T(2,128)(2,1)} %reshape.71), calls=%async_computation.4 | async-start | bytes 1048576 | tf_op jit(solution)/shard_map/all_to_all | solution.py:77
  69.5 17.4 %all-to-all-done.4 = bf16[32,2,2,2048]{3,2,1,0:T(2,128)(2,1)S(1)} async-done(((bf16[32,2,2,2048]{3,2,1,0:T(2,128)(2,1)}), bf16[32,2,2,2048]{3,2,1,0:T(2,128)(2,1)S(1)}, u32[]{:S(2)}, u32[]{:S(2)}) %all-to-all-start.4) | async-done | bytes 524320 | tf_op jit(solution)/shard_map/all_to_all | solution.py:77
  87.0 5.5 %broadcast_in_dim.44 = bf16[32,2,8,2,2048]{4,3,0,2,1:T(2,128)(2,1)} broadcast(bf16[32,2,2,2048]{3,2,0,1:T(2,128)(2,1)S(1)} %copy.116), dimensions={0,1,3,4} | broadcast | bytes 4718592 | tf_op jit(solution)/shard_map/broadcast_in_dim | solution.py:82
  92.5 7.6 %all-to-all-start.3 = ((bf16[32,16,2,2048]{3,2,0,1:T(2,128)(2,1)}), bf16[32,16,2,2048]{3,2,0,1:T(2,128)(2,1)}, u32[]{:S(2)}, u32[]{:S(2)}) async-start(bf16[32,16,2,2048]{3,2,0,1:T(2,128)(2,1)} %bitcast.112), calls=%async_computation.3 | async-start | bytes 8388608 | tf_op jit(solution)/shard_map/all_to_all | solution.py:86
  100.4 3.2 broadcast_in_dim.45
  103.7 0.9 fusion.19
  104.6 0.9 fusion.18
  105.5 0.9 fusion.17
  106.4 0.9 fusion.16
  107.3 0.9 fusion.15
  108.1 0.9 fusion.14
  109.0 0.9 fusion.13
  109.9 0.9 fusion.12
  110.8 0.9 fusion.11
  111.6 0.9 fusion.10
  112.5 0.9 fusion.9
  113.4 0.9 fusion.8
  114.3 0.9 fusion.7
  115.2 0.9 fusion.6
  116.1 0.9 fusion.5
  117.0 0.9 fusion.4
  117.9 43.4 %all-to-all-done.3 = bf16[32,16,2,2048]{3,2,0,1:T(2,128)(2,1)} async-done(((bf16[32,16,2,2048]{3,2,0,1:T(2,128)(2,1)}), bf16[32,16,2,2048]{3,2,0,1:T(2,128)(2,1)}, u32[]{:S(2)}, u32[]{:S(2)}) %all-to-all-start.3) | async-done | bytes 4194336 | tf_op jit(solution)/shard_map/all_to_all | solution.py:86
  161.3 6.0 %all-to-all-start.5 = ((bf16[16,32,1,2,2048]{4,3,1,2,0:T(2,128)(2,1)}), bf16[16,32,1,2,2048]{4,3,1,2,0:T(2,128)(2,1)}, u32[]{:S(2)}, u32[]{:S(2)}) async-start(bf16[16,32,1,2,2048]{4,3,1,2,0:T(2,128)(2,1)} %fusion.4), calls=%async_computation.5 | async-start | bytes 8388608 | tf_op jit(solution)/shard_map/all_to_all | solution.py:9
  167.7 8.7 %copy.117 = bf16[32,16,2,2048]{3,2,1,0:T(2,128)(2,1)} copy(bf16[32,16,2,2048]{3,2,0,1:T(2,128)(2,1)} %all-to-all-done.3) | data formatting | bytes 8388608 | tf_op jit(solution)/shard_map/all_to_all | solution.py:86
  176.4 7.2 %reshape.70 = bf16[1024,2048]{1,0:T(8,128)(2,1)} reshape(bf16[32,16,2,2048]{3,2,1,0:T(2,128)(2,1)} %copy.117) | data formatting | bytes 8388608 | tf_op jit(solution)/shard_map/reshape | solution.py:28
  183.6 45.0 %all-to-all-done.5 = bf16[16,32,1,2,2048]{4,3,1,2,0:T(2,128)(2,1)} async-done(((bf16[16,32,1,2,2048]{4,3,1,2,0:T(2,128)(2,1)}), bf16[16,32,1,2,2048]{4,3,1,2,0:T(2,128)(2,1)}, u32[]{:S(2)}, u32[]{:S(2)}) %all-to-all-start.5) | async-done | bytes 4194336 | tf_op jit(solution)/shard_map/all_to_all | solution.py:9
  228.5 8.7 %copy.119 = bf16[32,16,1,2,2048]{4,3,1,0,2:T(2,128)(2,1)} copy(bf16[32,16,1,2,2048]{4,3,0,2,1:T(2,128)(2,1)} %bitcast.19) | data formatting | bytes 8388608 | tf_op jit(solution)/shard_map/reshape | solution.py:8
  237.2 7.5 %reshape_reshape.3 = bf16[1024,2048]{1,0:T(8,128)(2,1)} reshape(bf16[32,16,1,2,2048]{4,3,1,0,2:T(2,128)(2,1)} %copy.119) | data formatting | bytes 8388608 | tf_op jit(solution)/shard_map/reshape;reshape | solution.py:27
  244.7 3.9 fusion.22
  248.6 1.5 fusion.21
  250.2 1.7 multiply_reduce_fusion
  251.9 1.3 fusion.23
  253.2 3.2 add_convert_fusion
  256.4 7.7 %reshape.74 = bf16[32,16,2,2048]{3,2,1,0:T(2,128)(2,1)} reshape(bf16[1024,2048]{1,0:T(8,128)(2,1)} %add_convert_fusion) | data formatting | bytes 8388608 | tf_op jit(solution)/shard_map/reshape | solution.py:100
  264.1 8.0 %copy.120 = bf16[32,16,2,2048]{3,2,0,1:T(2,128)(2,1)} copy(bf16[32,16,2,2048]{3,2,1,0:T(2,128)(2,1)} %reshape.74) | data formatting | bytes 8388608 | tf_op jit(solution)/shard_map/reshape | solution.py:100
  272.1 5.9 %all-to-all-start.6 = ((bf16[32,16,2,2048]{3,2,0,1:T(2,128)(2,1)}), bf16[32,16,2,2048]{3,2,0,1:T(2,128)(2,1)}, u32[]{:S(2)}, u32[]{:S(2)}) async-start(bf16[32,16,2,2048]{3,2,0,1:T(2,128)(2,1)} %copy.120), calls=%async_computation.6 | async-start | bytes 8388608 | tf_op jit(solution)/shard_map/all_to_all | solution.py:99
  278.5 101.7 %psum.7 = f32[2,32,16,2]{1,3,2,0:T(2,128)S(1)} all-reduce(f32[2,32,16,2]{1,3,2,0:T(2,128)S(1)} %broadcast_select_fusion.2), channel_id=1, replica_groups=mesh['pipe'=32,'expert'=16] {'expert'}, use_global_device_ids=true, to_apply=%region_2.4 | all-reduce | flops 2048 | bytes 16384 | tf_op jit(solution)/shard_map/psum | solution.py:96
  380.2 0.7 copy.123
  380.9 6.6 %all-to-all-start.8 = ((f32[32,2,2]{2,1,0:T(2,128)}), f32[32,2,2]{2,1,0:T(2,128)S(1)}, u32[]{:S(2)}, u32[]{:S(2)}) async-start(f32[32,2,2]{2,1,0:T(2,128)} %copy.123), calls=%async_computation.8 | async-start | bytes 65536 | tf_op jit(solution)/shard_map/all_to_all | solution.py:114
  387.5 6.3 %convert_reduce_fusion = f32[32,2,2,2048]{3,2,0,1:T(2,128)S(1)} fusion(bf16[32,16,2,2048]{3,2,0,1:T(2,128)(2,1)} %all-to-all-done.6), kind=kLoop, calls=%fused_computation.2 | loop fusion | flops 3932160 | bytes 5242880 | tf_op jit(solution)/shard_map/reduce_sum | solution.py:106
  393.9 1.1 copy.121
  395.0 0.9 all-to-all-done.8
  395.8 10.8 %all-to-all-start.7 = ((f32[32,2,2,2048]{3,2,1,0:T(2,128)}), f32[32,2,2,2048]{3,2,1,0:T(2,128)S(1)}, u32[]{:S(2)}, u32[]{:S(2)}) async-start(f32[32,2,2,2048]{3,2,1,0:T(2,128)} %copy.121), calls=%async_computation.7 | async-start | bytes 2097152 | tf_op jit(solution)/shard_map/all_to_all | solution.py:113
  406.6 4.4 convolution_convert_fusion.1
  411.1 2.1 convolution_convert_fusion
  413.2 1.9 fusion.2
  415.1 0.6 copy.125
  415.7 30.8 %all-to-all-done.7 = f32[32,2,2,2048]{3,2,1,0:T(2,128)S(1)} async-done(((f32[32,2,2,2048]{3,2,1,0:T(2,128)}), f32[32,2,2,2048]{3,2,1,0:T(2,128)S(1)}, u32[]{:S(2)}, u32[]{:S(2)}) %all-to-all-start.7) | async-done | bytes 1048608 | tf_op jit(solution)/shard_map/all_to_all | solution.py:113
  446.5 0.7 reshape.77
  447.2 1.5 convolution_convert_fusion.2
  (33 shorter events, 2.0 us)
Async XLA Ops:
  0.6 244.1 %copy-start = (bf16[2048,128]{1,0:T(8,128)(2,1)S(1)}, bf16[2048,128]{1,0:T(8,128)(2,1)}, u32[]{:S(2)}) copy-start(bf16[2048,128]{1,0:T(8,128)(2,1)} %param.13) | copy-start | bytes 1572868
  0.6 19.6 %copy-start.3 = (bf16[128,2048]{1,0:T(8,128)(2,1)S(1)}, bf16[128,2048]{1,0:T(8,128)(2,1)}, u32[]{:S(2)}) copy-start(bf16[128,2048]{1,0:T(8,128)(2,1)} %param.10) | copy-start | bytes 1572868
  2.1 22.9 %all-to-all-start = ((bf16[32,2,2]{1,2,0:T(2,128)(2,1)}), bf16[32,2,2]{1,2,0:T(2,128)(2,1)S(1)}, u32[]{:S(2)}, u32[]{:S(2)}) async-start(bf16[32,2,2]{1,2,0:T(2,128)(2,1)} %copy.112), calls=%async_computation | async-start | bytes 32768 | tf_op jit(solution)/shard_map/all_to_all | solution.py:79
  25.7 10.4 %all-to-all-start.1 = ((bf16[32,16,2]{0,2,1:T(2,128)(2,1)}), bf16[32,16,2]{0,2,1:T(2,128)(2,1)S(1)}, u32[]{:S(2)}, u32[]{:S(2)}) async-start(bf16[32,16,2]{0,2,1:T(2,128)(2,1)} %bitcast), calls=%async_computation.1 | async-start | bytes 16384 | tf_op jit(solution)/shard_map/all_to_all | solution.py:87
  36.1 26.4 %all-to-all-start.2 = ((bf16[32,2,2,2048]{3,2,1,0:T(2,128)(2,1)}), bf16[32,2,2,2048]{3,2,1,0:T(2,128)(2,1)S(1)}, u32[]{:S(2)}, u32[]{:S(2)}) async-start(bf16[32,2,2,2048]{3,2,1,0:T(2,128)(2,1)} %reshape.68), calls=%async_computation.2 | async-start | bytes 1048576 | tf_op jit(solution)/shard_map/all_to_all | solution.py:78
  62.6 24.4 %all-to-all-start.4 = ((bf16[32,2,2,2048]{3,2,1,0:T(2,128)(2,1)}), bf16[32,2,2,2048]{3,2,1,0:T(2,128)(2,1)S(1)}, u32[]{:S(2)}, u32[]{:S(2)}) async-start(bf16[32,2,2,2048]{3,2,1,0:T(2,128)(2,1)} %reshape.71), calls=%async_computation.4 | async-start | bytes 1048576 | tf_op jit(solution)/shard_map/all_to_all | solution.py:77
  92.5 68.8 %all-to-all-start.3 = ((bf16[32,16,2,2048]{3,2,0,1:T(2,128)(2,1)}), bf16[32,16,2,2048]{3,2,0,1:T(2,128)(2,1)}, u32[]{:S(2)}, u32[]{:S(2)}) async-start(bf16[32,16,2,2048]{3,2,0,1:T(2,128)(2,1)} %bitcast.112), calls=%async_computation.3 | async-start | bytes 8388608 | tf_op jit(solution)/shard_map/all_to_all | solution.py:86
  161.3 67.2 %all-to-all-start.5 = ((bf16[16,32,1,2,2048]{4,3,1,2,0:T(2,128)(2,1)}), bf16[16,32,1,2,2048]{4,3,1,2,0:T(2,128)(2,1)}, u32[]{:S(2)}, u32[]{:S(2)}) async-start(bf16[16,32,1,2,2048]{4,3,1,2,0:T(2,128)(2,1)} %fusion.4), calls=%async_computation.5 | async-start | bytes 8388608 | tf_op jit(solution)/shard_map/all_to_all | solution.py:9
  237.2 11.4 %copy-start.6 = (bf16[2048,128]{1,0:T(8,128)(2,1)S(1)}, bf16[2048,128]{1,0:T(8,128)(2,1)}, u32[]{:S(2)}) copy-start(bf16[2048,128]{1,0:T(8,128)(2,1)} %param.14) | copy-start | bytes 1572868
  244.7 3.9 copy-start.1
  244.7 5.4 %copy-start.4 = (bf16[1024,2048]{1,0:T(8,128)(2,1)S(1)}, bf16[1024,2048]{1,0:T(8,128)(2,1)}, u32[]{:S(2)}) copy-start(bf16[1024,2048]{1,0:T(8,128)(2,1)} %reshape.70) | copy-start | bytes 12582916
  244.7 5.4 %copy-start.7 = (bf16[128,2048]{1,0:T(8,128)(2,1)S(1)}, bf16[128,2048]{1,0:T(8,128)(2,1)}, u32[]{:S(2)}) copy-start(bf16[128,2048]{1,0:T(8,128)(2,1)} %param.15) | copy-start | bytes 1572868
  272.1 108.9 %all-to-all-start.6 = ((bf16[32,16,2,2048]{3,2,0,1:T(2,128)(2,1)}), bf16[32,16,2,2048]{3,2,0,1:T(2,128)(2,1)}, u32[]{:S(2)}, u32[]{:S(2)}) async-start(bf16[32,16,2,2048]{3,2,0,1:T(2,128)(2,1)} %copy.120), calls=%async_computation.6 | async-start | bytes 8388608 | tf_op jit(solution)/shard_map/all_to_all | solution.py:99
  380.9 14.9 %all-to-all-start.8 = ((f32[32,2,2]{2,1,0:T(2,128)}), f32[32,2,2]{2,1,0:T(2,128)S(1)}, u32[]{:S(2)}, u32[]{:S(2)}) async-start(f32[32,2,2]{2,1,0:T(2,128)} %copy.123), calls=%async_computation.8 | async-start | bytes 65536 | tf_op jit(solution)/shard_map/all_to_all | solution.py:114
  395.8 50.7 %all-to-all-start.7 = ((f32[32,2,2,2048]{3,2,1,0:T(2,128)}), f32[32,2,2,2048]{3,2,1,0:T(2,128)S(1)}, u32[]{:S(2)}, u32[]{:S(2)}) async-start(f32[32,2,2,2048]{3,2,1,0:T(2,128)} %copy.121), calls=%async_computation.7 | async-start | bytes 2097152 | tf_op jit(solution)/shard_map/all_to_all | solution.py:113
  406.6 4.5 copy-start.2
  406.6 6.6 %copy-start.5 = (bf16[1024,2048]{1,0:T(8,128)(2,1)S(1)}, bf16[1024,2048]{1,0:T(8,128)(2,1)}, u32[]{:S(2)}) copy-start(bf16[1024,2048]{1,0:T(8,128)(2,1)} %reshape.70) | copy-start | bytes 12582916
